TPU v7x, 128 devices: a whole 4x4x4 slice. The times are simulated.
128 devices in a mesh: row: 8 (over z_hi, y), col: 8 (over x, core), dp: 2 (over z_lo).
Axes of the slice: x: 4, y: 4, z: 4 (z_hi: 2, z_lo: 2; z = z_hi * 2 + z_lo), core: 2. Of those that a mesh axis runs over, the one named last changes fastest.
Arguments:
- tokens: bfloat16 [2048, 8192], P(('dp', 'row'), 'col'), may hold values from -6 to 6
- w_in: bfloat16 [8192, 14336], P('col', 'row'), may hold values from -0.0625 to 0.0625
- w_out: bfloat16 [14336, 8192], P('row', 'col'), may hold values from -0.046875 to 0.046875
- spike_gain: float32 [14336], P('row'), may hold values from 1 to 4
- cotangent: bfloat16 [2048, 8192], P(('dp', 'row'), 'col'), may hold values from -1.5 to 1.5
Outputs:
- output: bfloat16 [2048, 8192], P(('dp', 'row'), 'col')
- grad_tokens: bfloat16 [2048, 8192], P(('dp', 'row'), 'col')
- grad_w_in: bfloat16 [8192, 14336], P('col', 'row')
- grad_w_out: bfloat16 [14336, 8192], P('row', 'col')
All inputs are finite; a program needn't handle non-finite values.
Results may differ from a plain program's by a relative error of at most 0.035.
Values may be sent and summed in bfloat16 or wider, within the bound.
A program may use at most 128 MiB of HBM per device.

v0:
```python
import jax
import jax.numpy as jnp
from jax import lax
from jax.sharding import PartitionSpec as P

LEVELS = 4


sharpness = 4.0


def spike_parts(potential, gain):
    scaled = potential * gain[None, :]
    total = jnp.zeros_like(scaled)
    slope = jnp.zeros_like(scaled)
    for level in range(LEVELS):
        sig = jax.nn.sigmoid(sharpness * (scaled - (level + 0.5)))
        total = total + sig
        slope = slope + sig * (1.0 - sig)
    return (total, slope * (sharpness * gain[None, :]))


def times_transposed(left, right):
    return lax.dot_general(
        left, right, (((1,), (1,)), ((), ())), preferred_element_type=jnp.float32
    )


def over_tokens(left, right):
    return lax.dot_general(
        left, right, (((0,), (0,)), ((), ())), preferred_element_type=jnp.float32
    )


def shards(tokens, w_in, w_out, spike_gain, cotangent):
    tok_all = lax.all_gather(tokens, "row", axis=0, tiled=True)
    potential = lax.psum_scatter(
        jnp.dot(tok_all, w_in, preferred_element_type=jnp.float32).astype(jnp.bfloat16),
        "col",
        scatter_dimension=0,
        tiled=True,
    ).astype(jnp.float32)
    total, slope = spike_parts(potential, spike_gain)
    spikes = total.astype(jnp.bfloat16)
    spike_all = lax.all_gather(spikes, "col", axis=0, tiled=True)
    output = lax.psum_scatter(
        jnp.dot(spike_all, w_out, preferred_element_type=jnp.float32).astype(jnp.bfloat16),
        "row",
        scatter_dimension=0,
        tiled=True,
    )
    cot_all = lax.all_gather(cotangent, "row", axis=0, tiled=True)
    grad_spikes = lax.psum_scatter(
        times_transposed(cot_all, w_out).astype(jnp.bfloat16),
        "col",
        scatter_dimension=0,
        tiled=True,
    ).astype(jnp.float32)
    grad_potential = (grad_spikes * slope).astype(jnp.bfloat16)
    grad_all = lax.all_gather(grad_potential, "col", axis=0, tiled=True)
    grad_tokens = lax.psum_scatter(
        times_transposed(grad_all, w_in).astype(jnp.bfloat16),
        "row",
        scatter_dimension=0,
        tiled=True,
    )
    grad_w_in = over_tokens(tok_all, grad_all)
    grad_w_out = over_tokens(spike_all, cot_all)
    grad_w_in, grad_w_out = (
        lax.psum(grad_w_in.astype(jnp.bfloat16), "dp").astype(jnp.float32),
        lax.psum(grad_w_out.astype(jnp.bfloat16), "dp").astype(jnp.float32),
    )
    return (output, grad_tokens, grad_w_in.astype(jnp.bfloat16), grad_w_out.astype(jnp.bfloat16))


def solution(mesh):
    placed = (
        P(("dp", "row"), "col"),
        P("col", "row"),
        P("row", "col"),
        P("row"),
        P(("dp", "row"), "col"),
    )
    return jax.shard_map(
        shards,
        mesh=mesh,
        in_specs=placed,
        out_specs=(
            P(("dp", "row"), "col"),
            P(("dp", "row"), "col"),
            P("col", "row"),
            P("row", "col"),
        ),
        check_vma=False,
    )
```

profile of v0, /device:TPU:0, one launch (start us, length us, event | category | flops | bytes accessed | tf_op | source)
XLA Modules:
  0.0 627.4 jit_solution(12342968737964051404)
XLA Ops:
  7.2 0.0 all-gather.9.cloned.1.call-start
  7.2 0.7 all-gather.9.cloned.1.call-update
  7.9 0.0 all-gather.5.cloned.1.call-start
  7.9 0.7 all-gather.5.cloned.1.call-update
  8.6 0.0 reduce-scatter.9.cloned.1.call-start
  8.7 59.2 %all-gather.9.cloned.1.call-done = bf16[1024,1024]{1,0:T(8,128)(2,1)} async-done(((bf16[128,1024]{1,0:T(8,128)(2,1)}), bf16[1024,1024]{1,0:T(8,128)(2,1)}) %all-gather.9.cloned.1.call-update) | async-done | bytes 2097168 | tf_op jit(solution)/shard_map/all_gather | solution.py:52
  67.8 8.5 %convolution_convert_fusion.2 = bf16[1024,1792]{1,0:T(8,128)(2,1)} fusion(bf16[1024,1024]{1,0:T(8,128)(2,1)} %all-gather.9.cloned.1.call-done, bf16[1792,1024]{1,0:T(8,128)(2,1)} %param.7), kind=kOutput, calls=%fused_computation.2 | convolution fusion | flops 3759931392 | bytes 9437184 | tf_op jit(solution)/shard_map/dot_general | solution.py:24
  76.4 0.0 reduce-scatter.5.cloned.1.call-start
  76.4 47.4 %all-gather.5.cloned.1.call-done = bf16[1024,1024]{1,0:T(8,128)(2,1)} async-done(((bf16[128,1024]{1,0:T(8,128)(2,1)}), bf16[1024,1024]{1,0:T(8,128)(2,1)}) %all-gather.5.cloned.1.call-update) | async-done | bytes 2097168 | tf_op jit(solution)/shard_map/all_gather | solution.py:36
  123.9 8.5 %convolution_convert_fusion.3 = bf16[1024,1792]{1,0:T(8,128)(2,1)} fusion(bf16[1024,1024]{1,0:T(8,128)(2,1)} %all-gather.5.cloned.1.call-done, bf16[1024,1792]{1,0:T(8,128)(2,1)} %param.6), kind=kOutput, calls=%fused_computation.3 | convolution fusion | flops 3759931392 | bytes 9437184 | tf_op jit(solution)/shard_map/dot_general | solution.py:38
  132.4 0.0 all-gather.7.cloned.1.call-start
  132.4 0.6 copy-done
  133.0 29.4 %reduce-scatter.9.cloned.1.call-done = bf16[128,1792]{1,0:T(8,128)(2,1)} async-done(((bf16[1024,1792]{1,0:T(8,128)(2,1)}), bf16[128,1792]{1,0:T(8,128)(2,1)}) %reduce-scatter.9.cloned.1.call-update) | async-done | bytes 458768 | tf_op jit(solution)/shard_map/reduce_scatter | solution.py:53
  162.4 38.6 %reduce-scatter.5.cloned.1.call-done = bf16[128,1792]{1,0:T(8,128)(2,1)} async-done(((bf16[1024,1792]{1,0:T(8,128)(2,1)}), bf16[128,1792]{1,0:T(8,128)(2,1)}) %reduce-scatter.5.cloned.1.call-update) | async-done | bytes 458768 | tf_op jit(solution)/shard_map/reduce_scatter | solution.py:37
  201.0 3.4 fusion.6
  204.4 0.0 all-gather.7.cloned.1.call-update
  204.4 0.0 all-gather.11.cloned.1.call-start
  204.4 0.5 all-gather.11.cloned.1.call-update
  205.0 0.2 all-reduce.3.cloned.1.call-start
  205.2 28.0 %all-gather.7.cloned.1.call-done = bf16[1024,1792]{1,0:T(8,128)(2,1)} async-done(((bf16[128,1792]{1,0:T(8,128)(2,1)}), bf16[1024,1792]{1,0:T(8,128)(2,1)}) %all-gather.7.cloned.1.call-update) | async-done | bytes 3670032 | tf_op jit(solution)/shard_map/all_gather | solution.py:45
  233.2 7.5 %convolution_convert_fusion = bf16[1792,1024]{1,0:T(8,128)(2,1)} fusion(bf16[1024,1792]{1,0:T(8,128)(2,1)} %all-gather.7.cloned.1.call-done, bf16[1024,1024]{1,0:T(8,128)(2,1)S(1)} %copy-done.1), kind=kOutput, calls=%fused_computation | convolution fusion | flops 3759931392 | bytes 9437184 | tf_op jit(solution)/shard_map/dot_general | solution.py:30
  240.7 24.5 %all-gather.11.cloned.1.call-done = bf16[1024,1792]{1,0:T(8,128)(2,1)} async-done(((bf16[128,1792]{1,0:T(8,128)(2,1)}), bf16[1024,1792]{1,0:T(8,128)(2,1)}) %all-gather.11.cloned.1.call-update) | async-done | bytes 3670032 | tf_op jit(solution)/shard_map/all_gather | solution.py:60
  265.2 8.6 %fusion = bf16[1024,1792]{0,1:T(8,128)(2,1)} fusion(bf16[1024,1792]{1,0:T(8,128)(2,1)} %all-gather.11.cloned.1.call-done, bf16[1024,1024]{1,0:T(8,128)(2,1)} %all-gather.5.cloned.1.call-done), kind=kOutput, calls=%fused_computation.4 | convolution fusion | flops 3759931392 | bytes 9437184 | tf_op jit(solution)/shard_map/dot_general | solution.py:30
  273.8 0.0 reduce-scatter.7.cloned.1.call-start
  273.8 8.4 %convolution_convert_fusion.5 = bf16[1024,1024]{1,0:T(8,128)(2,1)} fusion(bf16[1024,1792]{1,0:T(8,128)(2,1)} %all-gather.7.cloned.1.call-done, bf16[1792,1024]{1,0:T(8,128)(2,1)} %param.7), kind=kOutput, calls=%fused_computation.6 | convolution fusion | flops 3759144960 | bytes 9437184 | tf_op jit(solution)/shard_map/dot_general | solution.py:47
  282.2 0.0 reduce-scatter.11.cloned.1.call-start
  282.3 9.3 %convolution_convert_fusion.4 = bf16[1024,1024]{1,0:T(8,128)(2,1)} fusion(bf16[1024,1792]{1,0:T(8,128)(2,1)} %all-gather.11.cloned.1.call-done, bf16[1024,1792]{1,0:T(8,128)(2,1)} %param.6), kind=kOutput, calls=%fused_computation.5 | convolution fusion | flops 3759144960 | bytes 9437184 | tf_op jit(solution)/shard_map/dot_general | solution.py:24
  291.6 165.2 %all-reduce.3.cloned.1.call-done = (bf16[1024,1792]{0,1:T(8,128)(2,1)}, bf16[1792,1024]{1,0:T(8,128)(2,1)}) async-done(((bf16[1024,1792]{0,1:T(8,128)(2,1)}, bf16[1792,1024]{1,0:T(8,128)(2,1)}), (bf16[1024,1792]{0,1:T(8,128)(2,1)}, bf16[1792,1024]{1,0:T(8,128)(2,1)})) %all-reduce.3.cloned.1.call-update) | async-done | bytes 7340048 | tf_op jit(solution)/shard_map/psum | solution.py:70
  456.8 5.9 copy.9
  462.7 75.5 %reduce-scatter.7.cloned.1.call-done = bf16[128,1024]{1,0:T(8,128)(2,1)} async-done(((bf16[1024,1024]{1,0:T(8,128)(2,1)}), bf16[128,1024]{1,0:T(8,128)(2,1)}) %reduce-scatter.7.cloned.1.call-update) | async-done | bytes 262160 | tf_op jit(solution)/shard_map/reduce_scatter | solution.py:46
  538.2 78.4 %reduce-scatter.11.cloned.1.call-done = bf16[128,1024]{1,0:T(8,128)(2,1)} async-done(((bf16[1024,1024]{1,0:T(8,128)(2,1)}), bf16[128,1024]{1,0:T(8,128)(2,1)}) %reduce-scatter.11.cloned.1.call-update) | async-done | bytes 262160 | tf_op jit(solution)/shard_map/reduce_scatter | solution.py:61
  616.6 4.2 copy.12
  (9 shorter events, 0.1 us)
Async XLA Ops:
  7.2 60.7 %all-gather.9.cloned.1.call-start = ((), (), s32[]{:S(2)}) async-start(), calls=%async_computation.8 | async-start | bytes 2359296 | tf_op jit(solution)/shard_map/all_gather | solution.py:52
  7.9 116.0 %all-gather.5.cloned.1.call-start = ((), (), s32[]{:S(2)}) async-start(), calls=%async_computation.4 | async-start | bytes 2359296 | tf_op jit(solution)/shard_map/all_gather | solution.py:36
  8.6 153.7 %reduce-scatter.9.cloned.1.call-start = ((), (), s32[]{:S(2)}) async-start(), calls=%async_computation.9 | async-start | bytes 4128768 | tf_op jit(solution)/shard_map/reduce_scatter | solution.py:53
  76.4 124.6 %reduce-scatter.5.cloned.1.call-start = ((), (), s32[]{:S(2)}) async-start(), calls=%async_computation.5 | async-start | bytes 4128768 | tf_op jit(solution)/shard_map/reduce_scatter | solution.py:37
  132.3 0.7 copy-start
  132.3 100.9 %copy-start.1 = (bf16[1024,1024]{1,0:T(8,128)(2,1)S(1)}, bf16[1024,1024]{1,0:T(8,128)(2,1)}, u32[]{:S(2)}) copy-start(bf16[1024,1024]{1,0:T(8,128)(2,1)} %all-gather.9.cloned.1.call-done) | copy-start | bytes 6291460
  132.4 100.9 %all-gather.7.cloned.1.call-start = ((), (), s32[]{:S(2)}) async-start(), calls=%async_computation.6 | async-start | bytes 4128768 | tf_op jit(solution)/shard_map/all_gather | solution.py:45
  204.4 60.8 %all-gather.11.cloned.1.call-start = ((), (), s32[]{:S(2)}) async-start(), calls=%async_computation.10 | async-start | bytes 4128768 | tf_op jit(solution)/shard_map/all_gather | solution.py:60
  205.0 251.8 %all-reduce.3.cloned.1.call-start = ((), (), s32[]{:S(2)}) async-start(), calls=%async_computation.12 | async-start | bytes 14680064 | tf_op jit(solution)/shard_map/psum | solution.py:70
  273.8 264.4 %reduce-scatter.7.cloned.1.call-start = ((), (), s32[]{:S(2)}) async-start(), calls=%async_computation.7 | async-start | bytes 2359296 | tf_op jit(solution)/shard_map/reduce_scatter | solution.py:46
  282.2 334.3 %reduce-scatter.11.cloned.1.call-start = ((), (), s32[]{:S(2)}) async-start(), calls=%async_computation.11 | async-start | bytes 2359296 | tf_op jit(solution)/shard_map/reduce_scatter | solution.py:61
Sparse Core Ops, SparseCore 0:
  10.3 57.4 all-gather.8
  70.2 53.6 all-gather.4
  126.9 35.4 reduce-scatter.8
  165.2 35.7 reduce-scatter.4
  204.5 28.6 all-gather.6
  235.3 29.8 all-gather.10
  273.9 182.8 all-reduce.2
  461.6 76.5 reduce-scatter.6
  542.5 73.9 reduce-scatter.10
where the time goes:
time: 628 us; the launch traced here: 627 us
  waiting for transfers between devices  548 us (87%)
  matrix products  50.7 us (8%)
  between operations  13.8 us (2%)
  local copies, waits for them, and re-layouts  10.8 us (2%)
    psum x1, waiting for transfers between devices, shards(): lax.psum(grad_w_in.astype(jnp.bfloat16), 'dp').astype(jnp.float32)  165 us
    reduce_scatter x1, waiting for transfers between devices, shards(): lax.psum_scatter(times_transposed(grad_all, w_in).astype(jnp.bfloat16), '...  78.4 us
    reduce_scatter x1, waiting for transfers between devices, shards(): lax.psum_scatter(jnp.dot(spike_all, w_out, preferred_element_type=jnp.flo...  75.5 us
    all_gather x1, waiting for transfers between devices, shards(): cot_all = lax.all_gather(cotangent, 'row', axis=0, tiled=True)  59.2 us
    all_gather x1, waiting for transfers between devices, shards(): tok_all = lax.all_gather(tokens, 'row', axis=0, tiled=True)  47.4 us
    reduce_scatter x1, waiting for transfers between devices, shards(): lax.psum_scatter(jnp.dot(tok_all, w_in, preferred_element_type=jnp.float3...  38.6 us
    reduce_scatter x1, waiting for transfers between devices, shards(): lax.psum_scatter(times_transposed(cot_all, w_out).astype(jnp.bfloat16), '...  29.4 us
    all_gather x1, waiting for transfers between devices, shards(): spike_all = lax.all_gather(spikes, 'col', axis=0, tiled=True)  28 us
  transfers between devices with their start and end apart: 9, of which 9 were waited for; matrix products, arithmetic and copies ran while one was open for 8% of the time, Pallas kernels for 0%

commit v1 on v0

v1 whole, which is shorter than its diff:
```python
import jax
import jax.numpy as jnp
from jax import lax
from jax.experimental import pallas as pl
from jax.experimental.pallas import tpu as pltpu
from jax.sharding import PartitionSpec as P

LEVELS = 4
SHARP = 4.0
BF = jnp.bfloat16
F32 = jnp.float32
FEAT, HID, BLK = 1024, 1792, 128
SUB = 32
TILE = 256

NAMES = (
    ["za", "zb", "zc", "zd", "ze", "zf"]
    + ["ya", "yb", "yc", "yd", "ye", "yf", "yg", "yh", "oa", "ob", "oc", "od"]
    + [f"{n}{k}" for k in range(4) for n in (
        "r1", "r2p", "r2m", "r3p", "r3m",
        "gp", "gm", "gd", "g2p", "g2m", "g3",
        "hp", "hm", "h2p", "h2m", "h3")]
    + [f"{n}{k}" for k in range(2) for n in ("d2p", "d2m", "dep", "dem", "dlp", "dlm", "dz")]
)
INDEX = {name: i for i, name in enumerate(NAMES)}


def nn(a, b):
    return lax.dot_general(a, b, (((1,), (0,)), ((), ())), preferred_element_type=F32)


def nt(a, b):
    return lax.dot_general(a, b, (((1,), (1,)), ((), ())), preferred_element_type=F32)


def tn(a, b):
    return lax.dot_general(a, b, (((0,), (0,)), ((), ())), preferred_element_type=F32)


def kernel(tok_h, win_h, wout_h, gain_h, cot_h,
           out_h, gtok_h, gwin_h, gwout_h,
           win, wout, gain, TC, PP, RB, X2, X1, SG, OP, YB2, YB1, ZS, ZB, OS, WI, WO,
           ssem, rsem, lsem):
    row, col, d = lax.axis_index("row"), lax.axis_index("col"), lax.axis_index("dp")
    zh, y = row // 4, row % 4
    x, c = col // 2, col % 2
    z = 2 * zh + d
    sib = 1 - c

    def dev(xx=None, cc=None, yy=None, zz=None):
        xx = x if xx is None else xx
        cc = c if cc is None else cc
        yy = y if yy is None else yy
        zz = z if zz is None else zz
        return (4 * (zz // 2) + yy, 2 * xx + cc, zz % 2)

    xp, xm, xo = (x + 1) % 4, (x + 3) % 4, (x + 2) % 4
    yp, ym, yo = (y + 1) % 4, (y + 3) % 4, (y + 2) % 4
    zp, zm, zo = (z + 1) % 4, (z + 3) % 4, (z + 2) % 4
    to_xp, to_xm = dev(xx=xp), dev(xx=xm)
    to_yp, to_ym = dev(yy=yp), dev(yy=ym)
    to_zp, to_zm, to_zo = dev(zz=zp), dev(zz=zm), dev(zz=zo)
    to_sib = dev(cc=sib)
    to_dp = (row, col, 1 - d)

    sent = {}

    def send(name, src, dst, to):
        i = INDEX[name]
        copy = pltpu.make_async_remote_copy(
            src_ref=src, dst_ref=dst, send_sem=ssem.at[i], recv_sem=rsem.at[i],
            device_id=to, device_id_type=pl.DeviceIdType.MESH)
        copy.start()
        sent[name] = copy

    def got(*names):
        for name in names:
            sent[name].wait_recv()

    loads = [
        pltpu.make_async_copy(tok_h, TC.at[d, 0, y, zh], lsem.at[0]),
        pltpu.make_async_copy(cot_h, TC.at[d, 1, y, zh], lsem.at[1]),
        pltpu.make_async_copy(win_h, win, lsem.at[2]),
        pltpu.make_async_copy(wout_h, wout, lsem.at[3]),
        pltpu.make_async_copy(gain_h, gain, lsem.at[4]),
    ]
    for load in loads:
        load.start()
    barrier = pltpu.get_barrier_semaphore()
    for to in (to_xp, to_xm, to_yp, to_ym, to_zp, to_zm, to_zo, to_sib):
        pl.semaphore_signal(barrier, inc=1, device_id=to, device_id_type=pl.DeviceIdType.MESH)
    pl.semaphore_wait(barrier, 8)
    loads[0].wait()
    loads[1].wait()

    H0, H1 = pl.ds(0, 64), pl.ds(64, 64)

    def tc(dd, yy, hh, rows=None):
        return TC.at[dd, :, yy, hh] if rows is None else TC.at[dd, :, yy, hh, rows]

    def zslot(zz, rows):
        return tc(zz % 2, y, zz // 2, rows)

    def same(name, ref, to):
        send(name, ref, ref, to)

    same("za", zslot(z, H0), to_zp)
    same("zb", zslot(z, H1), to_zm)
    same("ya", tc(d, y, zh), to_yp)
    same("yb", tc(d, y, zh), to_ym)
    got("za")
    same("ze", zslot(zm, H0), to_zp)
    got("zb")
    same("zf", zslot(zp, H1), to_zm)
    same("zc", zslot(z, H1), to_zp)
    same("zd", zslot(z, H0), to_zm)
    for load in loads[2:]:
        load.wait()

    def chunk(k):
        return (y + k) % 4

    def first_products(k):
        yy = chunk(k)

        def tile(n, carry):
            cols = pl.ds(pl.multiple_of(n * TILE, TILE), TILE)
            a = TC[d, 0, yy].reshape(2 * BLK, FEAT)
            PP[k, 0, :, :, :, cols] = nn(a, win[:, cols]).astype(BF).reshape(2, 4, SUB, TILE)
            b = TC[d, 1, yy].reshape(2 * BLK, FEAT)
            PP[k, 1, :, :, :, cols] = nt(b, wout[cols, :]).astype(BF).reshape(2, 4, SUB, TILE)
            return carry

        lax.fori_loop(0, HID // TILE, tile, 0)
        send(f"r1{k}", PP.at[k, :, sib], RB.at[k], to_sib)

    def pair(k, kind, q):
        return PP[k, kind, c, q].astype(F32) + RB[k, kind, q].astype(F32)

    def reduce_far(k):
        got(f"r1{k}")
        for kind in range(2):
            PP[k, kind, c, xo] = pair(k, kind, xo).astype(BF)
        send(f"r2p{k}", PP.at[k, :, c, xo, pl.ds(0, 16)], X2.at[k, 0], to_xp)
        send(f"r2m{k}", PP.at[k, :, c, xo, pl.ds(16, 16)], X2.at[k, 1], to_xm)

    def reduce_near(k):
        for name, q, way, to in (("r2p", xp, 0, to_xp), ("r2m", xm, 1, to_xm)):
            got(f"{name}{k}")
            for kind in range(2):
                both = pair(k, kind, q).reshape(2, 16, HID)
                add = X2[k, way, kind].astype(F32)
                parts = [both[0], both[1]]
                parts[way] = parts[way] + add
                PP[k, kind, c, q] = jnp.stack(parts).reshape(SUB, HID).astype(BF)
            send(f"r3{'pm'[way]}{k}", PP.at[k, :, c, q], X1.at[k, way], to)

    def activate(k):
        got(f"r3p{k}", f"r3m{k}")
        yy = chunk(k)
        sums = [
            pair(k, kind, x) + X1[k, 0, kind].astype(F32) + X1[k, 1, kind].astype(F32)
            for kind in range(2)
        ]
        g = gain[...]
        scaled = sums[0] * g
        total = jnp.zeros_like(scaled)
        slope = jnp.zeros_like(scaled)
        for level in range(LEVELS):
            sig = jax.nn.sigmoid(SHARP * (scaled - (level + 0.5)))
            total = total + sig
            slope = slope + sig * (1.0 - sig)
        SG[d, 0, yy, c, x] = total.astype(BF)
        SG[d, 1, yy, c, x] = (sums[1] * (slope * (SHARP * g))).astype(BF)
        block = SG.at[d, :, yy, c, x]
        same(f"gp{k}", block, to_xp)
        same(f"gm{k}", block, to_xm)
        same(f"gd{k}", block, to_dp)

    def share_other(k):
        got(f"gd{k}")
        block = SG.at[1 - d, :, chunk(k), c, x]
        same(f"hp{k}", block, to_xp)
        same(f"hm{k}", block, to_xm)

    def forward(k, g, dd):
        yy = chunk(k)
        got(f"{g}p{k}")
        same(f"{g}2p{k}", SG.at[dd, :, yy, c, xm, pl.ds(0, 16)], to_xp)
        got(f"{g}m{k}")
        same(f"{g}2m{k}", SG.at[dd, :, yy, c, xp, pl.ds(16, 16)], to_xm)

    def to_sibling(k, g, dd):
        got(f"{g}2p{k}", f"{g}2m{k}")
        same(f"{g}3{k}", SG.at[dd, :, chunk(k), c], to_sib)

    def second_products(k):
        got(f"g3{k}")
        yy = chunk(k)

        def tile(n, carry):
            cols = pl.ds(pl.multiple_of(n * TILE, TILE), TILE)
            a = SG[d, 0, yy].reshape(2 * BLK, HID)
            OP[k, 0, :, :, cols] = nn(a, wout[:, cols]).astype(BF).reshape(2, BLK, TILE)
            b = SG[d, 1, yy].reshape(2 * BLK, HID)
            OP[k, 1, :, :, cols] = nt(b, win[cols, :]).astype(BF).reshape(2, BLK, TILE)
            return carry

        lax.fori_loop(0, FEAT // TILE, tile, 0)

    def out_far(kind):
        send(f"d2p{kind}", OP.at[2, kind, 0], YB2.at[0, kind], to_yp)
        send(f"d2m{kind}", OP.at[2, kind, 1], YB2.at[1, kind], to_ym)

    def out_early(kind):
        send(f"dep{kind}", OP.at[1, kind, 1], YB1.at[0, kind, 1], to_yp)
        send(f"dem{kind}", OP.at[3, kind, 0], YB1.at[1, kind, 0], to_ym)

    def strips(fn):
        def strip(i, carry):
            fn(pl.ds(pl.multiple_of(i * SUB, SUB), SUB))
            return carry
        lax.fori_loop(0, BLK // SUB, strip, 0)

    def out_late(kind):
        for name, k, half, way, to in (("d2p", 1, 0, 0, to_yp), ("d2m", 3, 1, 1, to_ym)):
            got(f"{name}{kind}")

            def add(rows):
                OP[k, kind, half, rows] = (
                    OP[k, kind, half, rows].astype(F32) + YB2[way, kind, rows].astype(F32)
                ).astype(BF)

            strips(add)
            send(f"dl{'pm'[way]}{kind}", OP.at[k, kind, half], YB1.at[way, kind, half], to)

    def out_sum(kind, half, rows):
        return (OP[0, kind, half, rows].astype(F32) + YB1[0, kind, half, rows].astype(F32)
                + YB1[1, kind, half, rows].astype(F32))

    def out_across(kind):
        got(f"dep{kind}", f"dem{kind}", f"dlp{kind}", f"dlm{kind}")

        def add(rows):
            ZS[kind, rows] = out_sum(kind, 1 - zh, rows).astype(BF)

        strips(add)
        send(f"dz{kind}", ZS.at[kind], ZB.at[kind], to_zo)

    stores = []

    def store(src, dst, i):
        copy = pltpu.make_async_copy(src, dst, lsem.at[i])
        copy.start()
        stores.append(copy)

    def out_final(kind):
        got(f"dz{kind}")

        def add(rows):
            OS[kind, rows] = (out_sum(kind, zh, rows) + ZB[kind, rows].astype(F32)).astype(BF)

        strips(add)
        store(OS.at[kind], (out_h, gtok_h)[kind], 5 + kind)

    def grad_in(dd, first):
        b = 4 * 2 * BLK

        def tile(n, carry):
            cols = pl.ds(pl.multiple_of(n * TILE, TILE), TILE)
            left = TC[dd, 0, :, :, :, cols].reshape(b, TILE)
            value = tn(left, SG[dd, 1].reshape(b, HID))
            if not first:
                value = value + WI[cols, :].astype(F32)
            WI[cols, :] = value.astype(BF)
            return carry

        lax.fori_loop(0, FEAT // TILE, tile, 0)

    def grad_out(dd, first):
        b = 4 * 2 * BLK

        def tile(n, carry):
            cols = pl.ds(pl.multiple_of(n * TILE, TILE), TILE)
            left = SG[dd, 0, :, :, :, :, cols].reshape(b, TILE)
            value = tn(left, TC[dd, 1].reshape(b, FEAT))
            if not first:
                value = value + WO[cols, :].astype(F32)
            WO[cols, :] = value.astype(BF)
            return carry

        lax.fori_loop(0, HID // TILE, tile, 0)

    got("ze", "zf")
    same("yc", tc(d, y, 1 - zh), to_yp)
    same("yd", tc(d, y, 1 - zh), to_ym)
    first_products(0)
    got("ya")
    same("ye", tc(d, ym, zh, H0), to_yp)
    got("yb")
    same("yf", tc(d, yp, zh, H1), to_ym)
    reduce_far(0)
    got("yc")
    same("yg", tc(d, ym, 1 - zh, H0), to_yp)
    got("yd")
    same("yh", tc(d, yp, 1 - zh, H1), to_ym)
    first_products(3)
    first_products(1)
    reduce_near(0)
    reduce_far(3)
    reduce_far(1)
    got("zc", "zd")
    activate(0)
    same("oa", TC.at[1 - d, :, y], to_yp)
    same("ob", TC.at[1 - d, :, y], to_ym)
    got("ye", "yf", "yg", "yh")
    first_products(2)
    reduce_near(3)
    reduce_near(1)
    reduce_far(2)
    forward(0, "g", d)
    activate(3)
    activate(1)
    reduce_near(2)
    to_sibling(0, "g", d)
    forward(3, "g", d)
    forward(1, "g", d)
    activate(2)
    second_products(0)
    to_sibling(3, "g", d)
    to_sibling(1, "g", d)
    forward(2, "g", d)
    got("oa")
    same("oc", TC.at[1 - d, :, ym, 0], to_yp)
    got("ob")
    same("od", TC.at[1 - d, :, yp, 1], to_ym)
    share_other(0)
    second_products(3)
    second_products(1)
    out_early(0)
    out_early(1)
    to_sibling(2, "g", d)
    share_other(3)
    share_other(1)
    forward(0, "h", 1 - d)
    second_products(2)
    out_far(0)
    out_far(1)
    share_other(2)
    to_sibling(0, "h", 1 - d)
    grad_out(d, True)
    forward(3, "h", 1 - d)
    forward(1, "h", 1 - d)
    out_late(0)
    out_late(1)
    to_sibling(3, "h", 1 - d)
    to_sibling(1, "h", 1 - d)
    forward(2, "h", 1 - d)
    grad_in(d, True)
    to_sibling(2, "h", 1 - d)
    out_across(0)
    out_across(1)
    got("oc", "od")
    got(*[f"h3{k}" for k in range(4)])
    grad_out(1 - d, False)
    store(WO, gwout_h, 7)
    out_final(0)
    out_final(1)
    grad_in(1 - d, False)
    store(WI, gwin_h, 8)
    for copy in stores:
        copy.wait()
    for name in NAMES:
        sent[name].wait_send()


def shards(tokens, w_in, w_out, spike_gain, cotangent):
    anywhere = pl.BlockSpec(memory_space=pl.ANY)
    vmem = pltpu.VMEM
    n = len(NAMES)
    return pl.pallas_call(
        kernel,
        out_shape=(
            jax.ShapeDtypeStruct((BLK, FEAT), BF),
            jax.ShapeDtypeStruct((BLK, FEAT), BF),
            jax.ShapeDtypeStruct((FEAT, HID), BF),
            jax.ShapeDtypeStruct((HID, FEAT), BF),
        ),
        in_specs=[anywhere] * 5,
        out_specs=[anywhere] * 4,
        scratch_shapes=[
            vmem((FEAT, HID), BF),
            vmem((HID, FEAT), BF),
            vmem((1, HID), F32),
            vmem((2, 2, 4, 2, BLK, FEAT), BF),
            vmem((4, 2, 2, 4, SUB, HID), BF),
            vmem((4, 2, 4, SUB, HID), BF),
            vmem((4, 2, 2, 16, HID), BF),
            vmem((4, 2, 2, SUB, HID), BF),
            vmem((2, 2, 4, 2, 4, SUB, HID), BF),
            vmem((4, 2, 2, BLK, FEAT), BF),
            vmem((2, 2, BLK, FEAT), BF),
            vmem((2, 2, 2, BLK, FEAT), BF),
            vmem((2, BLK, FEAT), BF),
            vmem((2, BLK, FEAT), BF),
            vmem((2, BLK, FEAT), BF),
            vmem((FEAT, HID), BF),
            vmem((HID, FEAT), BF),
            pltpu.SemaphoreType.DMA((n,)),
            pltpu.SemaphoreType.DMA((n,)),
            pltpu.SemaphoreType.DMA((9,)),
        ],
        compiler_params=pltpu.CompilerParams(
            collective_id=0, has_side_effects=True, vmem_limit_bytes=64 << 20
        ),
        name="spiking_block",
    )(tokens, w_in, w_out, spike_gain.reshape(1, HID), cotangent)


def solution(mesh):
    placed = (
        P(("dp", "row"), "col"),
        P("col", "row"),
        P("row", "col"),
        P("row"),
        P(("dp", "row"), "col"),
    )
    return jax.shard_map(
        shards,
        mesh=mesh,
        in_specs=placed,
        out_specs=(
            P(("dp", "row"), "col"),
            P(("dp", "row"), "col"),
            P("col", "row"),
            P("row", "col"),
        ),
        check_vma=False,
    )
```

time: 628 us -> 171 us (0.27)
  waiting for transfers between devices: 548 us -> 0 us
  Pallas kernels: 0 us -> 160 us
  matrix products: 50.7 us -> 0 us
  between operations: 13.8 us -> 0.64 us
    reduce_scatter x4 -> x0, waiting for transfers between devices: 222 us -> none  [the longest x1 78.4 us: shards(): lax.psum_scatter(times_transposed(grad_all, w_in).astype(jnp.bfloat16), '...]
    psum x1 -> x0, waiting for transfers between devices: 165 us -> none  [shards(): lax.psum(grad_w_in.astype(jnp.bfloat16), 'dp').astype(jnp.float32)]
    pallas_call x0 -> x1, Pallas kernels: none -> 160 us  [shards(): pl.pallas_call(kernel, out_shape=(jax.ShapeDtypeStruct((BLK, FEAT), BF),...]
    all_gather x4 -> x0, waiting for transfers between devices: 159 us -> none  [the longest x1 59.2 us: shards(): cot_all = lax.all_gather(cotangent, 'row', axis=0, tiled=True)]
    dot_general x6 -> x0, matrix products: 50.7 us -> none  [the longest x2 17.8 us: times_transposed(): lax.dot_general(left, right, (((1,), (1,)), ((), ())), preferred_element_...]
  transfers between devices with their start and end apart: 9 -> 0, of which waited for: 9 -> 0; matrix products, arithmetic and copies ran while one was open for 8% -> 0% of each run, Pallas kernels for 0% -> 0%
where the time goes in v1:
time: 171 us
  Pallas kernels  160 us (94%)
  local copies, waits for them, and re-layouts  10.7 us (6%)
    pallas_call x1, Pallas kernels, shards(): pl.pallas_call(kernel, out_shape=(jax.ShapeDtypeStruct((BLK, FEAT), BF),...  160 us
    unnamed x6, local copies, waits for them, and re-layouts  9.44 us

profile of v1, /device:TPU:0, one launch (start us, length us, event | category | flops | bytes accessed | tf_op | source)
XLA Modules:
  0.0 171.1 jit_solution(12031926319778047110)
XLA Ops:
  0.6 1.3 reshape.11.gain_h
  1.9 159.7 %spiking_block.1 = (bf16[128,1024]{1,0:T(8,128)(2,1)}, bf16[128,1024]{1,0:T(8,128)(2,1)}, bf16[1024,1792]{1,0:T(8,128)(2,1)}, bf16[1792,1024]{1,0:T(8,128)(2,1)}) custom-call(bf16[128,1024]{1,0:T(8,128)(2,1)} %tok_h.1, bf16[1024,1792]{1,0:T(8,128)(2,1)} %win_h.1, bf16[1792,1024]{1,0:T(8,128)(2,1)} %wout_h.1, f32[1,1792]{1,0:T(1,128)} %reshape.11.gain_h, ...), custom_call_target="tpu_custom_call" | custom-call | tf_op jit(solution)/shard_map/spiking_block/pallas_call | solution.py:381
  161.7 1.7 copy.13
  163.3 1.7 copy.14
  165.0 0.0 copy-start
  165.0 4.3 %copy.15 = bf16[1024,1792]{1,0:T(8,128)(2,1)} copy(bf16[1024,1792]{1,0:T(8,128)(2,1)} %get-tuple-element.10) | data formatting | bytes 7340032
  169.3 0.0 copy-done
  169.3 1.8 %copy.16 = bf16[1792,1024]{1,0:T(8,128)(2,1)} copy(bf16[1792,1024]{1,0:T(8,128)(2,1)S(1)} %copy-done) | data formatting | bytes 7340032
Async XLA Ops:
  165.0 4.3 %copy-start = (bf16[1792,1024]{1,0:T(8,128)(2,1)S(1)}, bf16[1792,1024]{1,0:T(8,128)(2,1)}, u32[]{:S(2)}) copy-start(bf16[1792,1024]{1,0:T(8,128)(2,1)} %get-tuple-element.11) | copy-start | bytes 11010052

commit v2 on v0

v2 whole, which is shorter than its diff:
```python
import jax
import jax.numpy as jnp
from jax import lax
from jax.experimental import pallas as pl
from jax.experimental.pallas import tpu as pltpu
from jax.sharding import PartitionSpec as P

LEVELS = 4
SHARP = 4.0
BF = jnp.bfloat16
F32 = jnp.float32
FEAT, HID, BLK = 1024, 1792, 128
SUB = 16
TILE = 256

DIRECT = (4, 0)

ORDER = [
    "I", "L", "A0", "B0", "Z2", "Z1", "C0", "D0", "A6", "Y3", "Y2", "A2", "Y1", "A1", "E0", "B6", "B2", "P6",
    "Z3", "P2", "B1", "F0", "A4", "M0", "C2", "C6", "B4", "P4", "C1", "D2", "D6", "C4", "A3", "Y5", "A7",
    "D1", "E2", "B3", "P3", "Y4", "P7", "B7", "E6", "D4", "E1", "F2", "C3", "A5", "P5", "M2", "C7", "J0",
    "B5", "F6", "E4", "M6", "F1", "D3", "D7", "M1", "C5", "F4", "M4", "E3", "E7", "D5", "G1", "G2", "G6",
    "F3", "F7", "M3", "M7", "N0", "E5", "H1", "H2", "H6", "G3", "F5", "J1", "G7", "M5", "U6", "V0", "H3",
    "U4", "U5", "U3", "H7", "J2", "U1", "J3", "U0", "N1", "J4", "J6", "V2", "J7", "V1", "G5", "V3", "v3",
    "u5", "u6", "Q1", "H5", "u1", "u0", "v0", "v1", "J5", "u4", "v2", "u3", "U2", "u2", "X", "Q0",
]


def nn(a, b):
    return lax.dot_general(a, b, (((1,), (0,)), ((), ())), preferred_element_type=F32)


def nt(a, b):
    return lax.dot_general(a, b, (((1,), (1,)), ((), ())), preferred_element_type=F32)


def tn(a, b):
    return lax.dot_general(a, b, (((0,), (0,)), ((), ())), preferred_element_type=F32)


def names():
    found = [f"z{a}" for a in "abcdef"] + [f"y{a}" for a in "abcdefgh"]
    for u in range(8):
        found += [f"{n}{u}" for n in (
            "r1", "r2p", "r2m", "r3ep", "r3em", "r3lp", "r3lm", "gp", "gm", "g2p", "g2m", "g3", "h3")]
        found += [f"hd{u}"] if u in DIRECT else [f"{n}{u}" for n in ("gd", "hp", "hm", "h2p", "h2m")]
        if u > 1:
            found += [f"opp{u}", f"opm{u}"]
    for r in range(2):
        found += [f"{n}{r}" for n in ("d2p", "d2m", "dep", "dem", "dlp", "dlm", "dz")]
    return found


NAMES = names()
INDEX = {name: i for i, name in enumerate(NAMES)}


def kernel(tok_h, win_h, wout_h, gain_h, cot_h,
           out_h, gtok_h, gwin_h, gwout_h,
           win, wout, gain, TC, PP, RB, X2, X1, SG, OP, YB2, YB1, ZS, ZB, OS, WI, WO,
           ssem, rsem, lsem):
    row, col, d = lax.axis_index("row"), lax.axis_index("col"), lax.axis_index("dp")
    zh, y = row // 4, row % 4
    x, c = col // 2, col % 2
    z = 2 * zh + d
    sib, e = 1 - c, 1 - d

    def dev(xx=None, cc=None, yy=None, zz=None):
        xx = x if xx is None else xx
        cc = c if cc is None else cc
        yy = y if yy is None else yy
        zz = z if zz is None else zz
        return (4 * (zz // 2) + yy, 2 * xx + cc, zz % 2)

    xp, xm, xo = (x + 1) % 4, (x + 3) % 4, (x + 2) % 4
    yp, ym = (y + 1) % 4, (y + 3) % 4
    zp, zm, zo = (z + 1) % 4, (z + 3) % 4, (z + 2) % 4
    to_xp, to_xm = dev(xx=xp), dev(xx=xm)
    to_yp, to_ym = dev(yy=yp), dev(yy=ym)
    to_zp, to_zm, to_zo = dev(zz=zp), dev(zz=zm), dev(zz=zo)
    to_sib = dev(cc=sib)
    to_dp = (row, col, e)

    sent = {}
    arrived = set()

    def send(name, src, dst, to):
        i = INDEX[name]
        copy = pltpu.make_async_remote_copy(
            src_ref=src, dst_ref=dst, send_sem=ssem.at[i], recv_sem=rsem.at[i],
            device_id=to, device_id_type=pl.DeviceIdType.MESH)
        copy.start()
        sent[name] = copy

    def same(name, ref, to):
        send(name, ref, ref, to)

    def got(*wanted):
        for name in wanted:
            if name not in arrived:
                arrived.add(name)
                sent[name].wait_recv()

    loads = [
        pltpu.make_async_copy(tok_h, TC.at[d, 0, y, zh], lsem.at[0]),
        pltpu.make_async_copy(cot_h, TC.at[d, 1, y, zh], lsem.at[1]),
        pltpu.make_async_copy(win_h, win, lsem.at[2]),
        pltpu.make_async_copy(wout_h, wout, lsem.at[3]),
        pltpu.make_async_copy(gain_h, gain, lsem.at[4]),
    ]
    stores = []

    def store(src, dst, i):
        copy = pltpu.make_async_copy(src, dst, lsem.at[i])
        copy.start()
        stores.append(copy)

    def at(u):
        return (y + u // 2) % 4, (zh + u % 2) % 2

    def both(dd, u):
        yy, hh = at(u)
        return TC.at[dd, :, yy, hh]

    def one(dd, kind, u):
        yy, hh = at(u)
        return TC.at[dd, kind, yy, hh]

    def zslot(zz, kind):
        return TC.at[zz % 2, kind, y, zz // 2]

    def start():
        for load in loads:
            load.start()
        barrier = pltpu.get_barrier_semaphore()
        for to in (to_xp, to_xm, to_yp, to_ym, to_zp, to_zm, to_zo, to_sib):
            pl.semaphore_signal(barrier, inc=1, device_id=to, device_id_type=pl.DeviceIdType.MESH)
        pl.semaphore_wait(barrier, 8)
        loads[0].wait()
        loads[1].wait()
        same("za", zslot(z, 0), to_zp)
        same("zb", zslot(z, 1), to_zm)
        same("ya", both(d, 0), to_yp)
        same("yb", both(d, 0), to_ym)

    def weights():
        for load in loads[2:]:
            load.wait()

    def along_z(n):
        if n == 1:
            got("za")
            same("ze", zslot(zm, 0), to_zp)
        elif n == 2:
            got("zb")
            same("zf", zslot(zp, 1), to_zm)
        else:
            same("zc", zslot(z, 1), to_zp)
            same("zd", zslot(z, 0), to_zm)

    def along_y(n):
        if n == 1:
            got("ze", "zf")
            same("yc", both(d, 1), to_yp)
            same("yd", both(d, 1), to_ym)
            return
        name, sends, kind, u, to = {
            2: ("ya", "ye", 0, 6, to_yp),
            3: ("yb", "yf", 1, 2, to_ym),
            4: ("yc", "yg", 0, 7, to_yp),
            5: ("yd", "yh", 1, 3, to_ym),
        }[n]
        got(name)
        same(sends, one(d, kind, u), to)

    SOURCES = {0: (), 1: ("ze", "zf"), 6: ("ya",), 2: ("yb",), 4: ("ye", "yf"),
               7: ("yc",), 3: ("yd",), 5: ("yg", "yh")}

    def inputs_across(u):
        got(*SOURCES[u])
        same(f"opp{u}", one(d, 0, u), to_zp)
        same(f"opm{u}", one(d, 1, u), to_zm)

    def first_products(u):
        got(*SOURCES[u])
        yy, hh = at(u)

        def tile(n, carry):
            cols = pl.ds(pl.multiple_of(n * TILE, TILE), TILE)
            shape = (2, 4, SUB, TILE)
            PP[u, 0, :, :, :, cols] = nn(TC[d, 0, yy, hh], win[:, cols]).astype(BF).reshape(shape)
            PP[u, 1, :, :, :, cols] = nt(TC[d, 1, yy, hh], wout[cols, :]).astype(BF).reshape(shape)
            return carry

        lax.fori_loop(0, HID // TILE, tile, 0)
        send(f"r1{u}", PP.at[u, :, sib], RB.at[u], to_sib)

    def pair(u, kind, q):
        return PP[u, kind, c, q].astype(F32) + RB[u, kind, q].astype(F32)

    def reduce_far(u):
        got(f"r1{u}")
        for name, kind, q, to, dst in (
            ("r2p", 0, xo, to_xp, X2.at[u, 0]),
            ("r2m", 1, xo, to_xm, X2.at[u, 1]),
            ("r3ep", 1, xp, to_xp, X1.at[u, 0, 1]),
            ("r3em", 0, xm, to_xm, X1.at[u, 1, 0]),
        ):
            PP[u, kind, c, q] = pair(u, kind, q).astype(BF)
            send(f"{name}{u}", PP.at[u, kind, c, q], dst, to)

    def reduce_near(u):
        for name, sends, kind, q, to in (
            ("r2p", "r3lp", 0, xp, to_xp),
            ("r2m", "r3lm", 1, xm, to_xm),
        ):
            got(f"{name}{u}")
            PP[u, kind, c, q] = (pair(u, kind, q) + X2[u, kind].astype(F32)).astype(BF)
            send(f"{sends}{u}", PP.at[u, kind, c, q], X1.at[u, kind, kind], to)

    def activate(u):
        got(f"r3ep{u}", f"r3em{u}", f"r3lp{u}", f"r3lm{u}")
        yy, hh = at(u)
        sums = [
            pair(u, kind, x) + X1[u, 0, kind].astype(F32) + X1[u, 1, kind].astype(F32)
            for kind in range(2)
        ]
        g = gain[...]
        scaled = sums[0] * g
        total = jnp.zeros_like(scaled)
        slope = jnp.zeros_like(scaled)
        for level in range(LEVELS):
            sig = jax.nn.sigmoid(SHARP * (scaled - (level + 0.5)))
            total = total + sig
            slope = slope + sig * (1.0 - sig)
        SG[d, 0, yy, hh, c, x] = total.astype(BF)
        SG[d, 1, yy, hh, c, x] = (sums[1] * (slope * (SHARP * g))).astype(BF)
        block = SG.at[d, :, yy, hh, c, x]
        same(f"gp{u}", block, to_xp)
        same(f"gm{u}", block, to_xm)
        if u not in DIRECT:
            same(f"gd{u}", block, to_dp)

    def forward(u, g, dd):
        yy, hh = at(u)
        got(f"{g}p{u}")
        same(f"{g}2p{u}", SG.at[dd, 0, yy, hh, c, xm], to_xp)
        got(f"{g}m{u}")
        same(f"{g}2m{u}", SG.at[dd, 1, yy, hh, c, xp], to_xm)

    def half_done(u):
        got(f"g2p{u}", f"g2m{u}")
        yy, hh = at(u)
        rows = SG.at[d, :, yy, hh, c]
        same(f"g3{u}", rows, to_sib)
        if u in DIRECT:
            same(f"hd{u}", rows, to_dp)

    def share_other(u):
        got(f"gd{u}")
        yy, hh = at(u)
        block = SG.at[e, :, yy, hh, c, x]
        same(f"hp{u}", block, to_xp)
        same(f"hm{u}", block, to_xm)

    def other_half_done(u):
        if u in DIRECT:
            got(f"hd{u}")
        else:
            got(f"h2p{u}", f"h2m{u}")
        yy, hh = at(u)
        same(f"h3{u}", SG.at[e, :, yy, hh, c], to_sib)

    def second_products(u):
        got(f"g3{u}")
        k, r = u // 2, u % 2
        yy, hh = at(u)

        def tile(n, carry):
            cols = pl.ds(pl.multiple_of(n * TILE, TILE), TILE)
            a = SG[d, 0, yy, hh].reshape(BLK, HID)
            OP[k, r, 0, :, cols] = nn(a, wout[:, cols]).astype(BF)
            b = SG[d, 1, yy, hh].reshape(BLK, HID)
            OP[k, r, 1, :, cols] = nt(b, win[cols, :]).astype(BF)
            return carry

        lax.fori_loop(0, FEAT // TILE, tile, 0)
        if k == 2:
            send(f"d2p{r}", OP.at[2, r, 0], YB2.at[r, 0], to_yp)
            send(f"d2m{r}", OP.at[2, r, 1], YB2.at[r, 1], to_ym)
        elif k == 1:
            send(f"dep{r}", OP.at[1, r, 1], YB1.at[r, 0, 1], to_yp)
        elif k == 3:
            send(f"dem{r}", OP.at[3, r, 0], YB1.at[r, 1, 0], to_ym)

    def strips(fn):
        def strip(i, carry):
            fn(pl.ds(pl.multiple_of(i * 32, 32), 32))
            return carry
        lax.fori_loop(0, BLK // 32, strip, 0)

    def out_late(r):
        for name, sends, k, kind, to in (
            ("d2p", "dlp", 1, 0, to_yp),
            ("d2m", "dlm", 3, 1, to_ym),
        ):
            got(f"{name}{r}")

            def add(rows):
                OP[k, r, kind, rows] = (
                    OP[k, r, kind, rows].astype(F32) + YB2[r, kind, rows].astype(F32)
                ).astype(BF)

            strips(add)
            send(f"{sends}{r}", OP.at[k, r, kind], YB1.at[r, kind, kind], to)

    def out_sum(kind, r, rows):
        return (OP[0, r, kind, rows].astype(F32) + YB1[r, 0, kind, rows].astype(F32)
                + YB1[r, 1, kind, rows].astype(F32))

    def finish(r):
        for kind in range(2):
            got(f"{('dlp', 'dep')[kind]}{r}", f"{('dem', 'dlm')[kind]}{r}")
            if r == 1:
                def add(rows):
                    ZS[kind, rows] = out_sum(kind, 1, rows).astype(BF)

                strips(add)
                send(f"dz{kind}", ZS.at[kind], ZB.at[kind], to_zo)
            else:
                got(f"dz{kind}")

                def add(rows):
                    OS[kind, rows] = (out_sum(kind, 0, rows) + ZB[kind, rows].astype(F32)).astype(BF)

                strips(add)
                store(OS.at[kind], (out_h, gtok_h)[kind], 5 + kind)

    def own_ready():
        got(*[f"g3{u}" for u in range(8)], *[s for u in range(8) for s in SOURCES[u]])

    def other_ready(units):
        got("za", "zb", "zc", "zd", *[f"h3{u}" for u in units])
        got(*[f"op{a}{u}" for u in units if u > 1 for a in "pm"])

    def out_left(dd, cols):
        return SG[dd, 0, :, :, :, :, :, cols].reshape(8 * BLK, TILE)

    def grad_out_own(n):
        own_ready()
        cols = slice(n * TILE, (n + 1) * TILE)
        WO[cols, :] = tn(out_left(d, cols), TC[d, 1].reshape(8 * BLK, FEAT)).astype(BF)

    def grad_in_own(n):
        own_ready()
        cols = slice(n * TILE, (n + 1) * TILE)
        left = TC[d, 0, :, :, :, cols].reshape(8 * BLK, TILE)
        WI[cols, :] = tn(left, SG[d, 1].reshape(8 * BLK, HID)).astype(BF)

    def grad_out_add(cols, ks):
        value = WO[cols, :].astype(F32)
        for k in ks:
            yy = (y + k) % 4
            left = SG[e, 0, yy, :, :, :, :, cols].reshape(2 * BLK, TILE)
            value = value + tn(left, TC[e, 1, yy].reshape(2 * BLK, FEAT))
        WO[cols, :] = value.astype(BF)

    def grad_in_add(cols, ks):
        value = WI[cols, :].astype(F32)
        for k in ks:
            yy = (y + k) % 4
            left = TC[e, 0, yy, :, :, cols].reshape(2 * BLK, TILE)
            value = value + tn(left, SG[e, 1, yy].reshape(2 * BLK, HID))
        WI[cols, :] = value.astype(BF)

    def grad_other(n, add):
        other_ready((0, 1, 2, 3, 6, 7))
        add(slice(n * TILE, (n + 1) * TILE), (0, 1, 3))

    def grad_last():
        other_ready(range(8))
        for add, rows, buffer, place, i in (
            (grad_out_add, HID, WO, gwout_h, 7),
            (grad_in_add, FEAT, WI, gwin_h, 8),
        ):
            def tile(n, carry):
                add(pl.ds(pl.multiple_of(n * TILE, TILE), TILE), (2,))
                return carry

            lax.fori_loop(0, rows // TILE, tile, 0)
            store(buffer, place, i)

    steps = {
        "I": start, "L": weights, "Z": along_z, "Y": along_y, "P": inputs_across,
        "A": first_products, "B": reduce_far, "C": reduce_near, "D": activate,
        "E": lambda u: forward(u, "g", d), "F": half_done,
        "G": share_other, "H": lambda u: forward(u, "h", e), "J": other_half_done,
        "M": second_products, "N": out_late, "Q": finish,
        "U": grad_out_own, "V": grad_in_own,
        "u": lambda n: grad_other(n, grad_out_add),
        "v": lambda n: grad_other(n, grad_in_add),
        "X": grad_last,
    }
    for step in ORDER:
        steps[step[0]](*[int(a) for a in step[1:]])
    for copy in stores:
        copy.wait()
    for name in NAMES:
        sent[name].wait_send()


def shards(tokens, w_in, w_out, spike_gain, cotangent):
    anywhere = pl.BlockSpec(memory_space=pl.ANY)
    vmem = pltpu.VMEM
    n = len(NAMES)
    return pl.pallas_call(
        kernel,
        out_shape=(
            jax.ShapeDtypeStruct((BLK, FEAT), BF),
            jax.ShapeDtypeStruct((BLK, FEAT), BF),
            jax.ShapeDtypeStruct((FEAT, HID), BF),
            jax.ShapeDtypeStruct((HID, FEAT), BF),
        ),
        in_specs=[anywhere] * 5,
        out_specs=[anywhere] * 4,
        scratch_shapes=[
            vmem((FEAT, HID), BF),
            vmem((HID, FEAT), BF),
            vmem((1, HID), F32),
            vmem((2, 2, 4, 2, BLK, FEAT), BF),
            vmem((8, 2, 2, 4, SUB, HID), BF),
            vmem((8, 2, 4, SUB, HID), BF),
            vmem((8, 2, SUB, HID), BF),
            vmem((8, 2, 2, SUB, HID), BF),
            vmem((2, 2, 4, 2, 2, 4, SUB, HID), BF),
            vmem((4, 2, 2, BLK, FEAT), BF),
            vmem((2, 2, BLK, FEAT), BF),
            vmem((2, 2, 2, BLK, FEAT), BF),
            vmem((2, BLK, FEAT), BF),
            vmem((2, BLK, FEAT), BF),
            vmem((2, BLK, FEAT), BF),
            vmem((FEAT, HID), BF),
            vmem((HID, FEAT), BF),
            pltpu.SemaphoreType.DMA((n,)),
            pltpu.SemaphoreType.DMA((n,)),
            pltpu.SemaphoreType.DMA((9,)),
        ],
        compiler_params=pltpu.CompilerParams(
            collective_id=0, has_side_effects=True, vmem_limit_bytes=64 << 20
        ),
        name="spiking_block",
    )(tokens, w_in, w_out, spike_gain.reshape(1, HID), cotangent)


def solution(mesh):
    placed = (
        P(("dp", "row"), "col"),
        P("col", "row"),
        P("row", "col"),
        P("row"),
        P(("dp", "row"), "col"),
    )
    return jax.shard_map(
        shards,
        mesh=mesh,
        in_specs=placed,
        out_specs=(
            P(("dp", "row"), "col"),
            P(("dp", "row"), "col"),
            P("col", "row"),
            P("row", "col"),
        ),
        check_vma=False,
    )
```

time: 628 us -> 142 us (0.23)
  waiting for transfers between devices: 548 us -> 0 us
  Pallas kernels: 0 us -> 130 us
  matrix products: 50.7 us -> 0 us
  between operations: 13.8 us -> 0.64 us
    reduce_scatter x4 -> x0, waiting for transfers between devices: 222 us -> none  [the longest x1 78.4 us: shards(): lax.psum_scatter(times_transposed(grad_all, w_in).astype(jnp.bfloat16), '...]
    psum x1 -> x0, waiting for transfers between devices: 165 us -> none  [shards(): lax.psum(grad_w_in.astype(jnp.bfloat16), 'dp').astype(jnp.float32)]
    all_gather x4 -> x0, waiting for transfers between devices: 159 us -> none  [the longest x1 59.2 us: shards(): cot_all = lax.all_gather(cotangent, 'row', axis=0, tiled=True)]
    pallas_call x0 -> x1, Pallas kernels: none -> 130 us  [shards(): pl.pallas_call(kernel, out_shape=(jax.ShapeDtypeStruct((BLK, FEAT), BF),...]
    dot_general x6 -> x0, matrix products: 50.7 us -> none  [the longest x2 17.8 us: times_transposed(): lax.dot_general(left, right, (((1,), (1,)), ((), ())), preferred_element_...]
  transfers between devices with their start and end apart: 9 -> 0, of which waited for: 9 -> 0; matrix products, arithmetic and copies ran while one was open for 8% -> 0% of each run, Pallas kernels for 0% -> 0%
where the time goes in v2:
time: 142 us; the launch traced here: 141 us
  Pallas kernels  130 us (92%)
  local copies, waits for them, and re-layouts  10.7 us (8%)
    pallas_call x1, Pallas kernels, shards(): pl.pallas_call(kernel, out_shape=(jax.ShapeDtypeStruct((BLK, FEAT), BF),...  130 us
    unnamed x6, local copies, waits for them, and re-layouts  9.44 us

profile of v2, /device:TPU:0, one launch (start us, length us, event | category | flops | bytes accessed | tf_op | source)
XLA Modules:
  0.0 141.3 jit_solution(6982043301556775786)
XLA Ops:
  0.6 1.3 reshape.11.gain_h
  1.9 129.9 %spiking_block.1 = (bf16[128,1024]{1,0:T(8,128)(2,1)}, bf16[128,1024]{1,0:T(8,128)(2,1)}, bf16[1024,1792]{1,0:T(8,128)(2,1)}, bf16[1792,1024]{1,0:T(8,128)(2,1)}) custom-call(bf16[128,1024]{1,0:T(8,128)(2,1)} %tok_h.1, bf16[1024,1792]{1,0:T(8,128)(2,1)} %win_h.1, bf16[1792,1024]{1,0:T(8,128)(2,1)} %wout_h.1, f32[1,1792]{1,0:T(1,128)} %reshape.11.gain_h, ...), custom_call_target="tpu_custom_call" | custom-call | tf_op jit(solution)/shard_map/spiking_block/pallas_call | solution.py:416
  131.9 1.7 %copy.13 = bf16[128,1024]{1,0:T(8,128)(2,1)} copy(bf16[128,1024]{1,0:T(8,128)(2,1)} %get-tuple-element.8) | data formatting | bytes 524288
  133.5 1.7 %copy.14 = bf16[128,1024]{1,0:T(8,128)(2,1)} copy(bf16[128,1024]{1,0:T(8,128)(2,1)} %get-tuple-element.9) | data formatting | bytes 524288
  135.2 0.0 copy-start
  135.2 4.3 %copy.15 = bf16[1024,1792]{1,0:T(8,128)(2,1)} copy(bf16[1024,1792]{1,0:T(8,128)(2,1)} %get-tuple-element.10) | data formatting | bytes 7340032
  139.5 0.0 copy-done
  139.5 1.8 %copy.16 = bf16[1792,1024]{1,0:T(8,128)(2,1)} copy(bf16[1792,1024]{1,0:T(8,128)(2,1)S(1)} %copy-done) | data formatting | bytes 7340032
Async XLA Ops:
  135.2 4.3 %copy-start = (bf16[1792,1024]{1,0:T(8,128)(2,1)S(1)}, bf16[1792,1024]{1,0:T(8,128)(2,1)}, u32[]{:S(2)}) copy-start(bf16[1792,1024]{1,0:T(8,128)(2,1)} %get-tuple-element.11) | copy-start | bytes 11010052

commit v3 on v2

--- a/solution.py
+++ b/solution.py
@@ -12,17 +12,18 @@
 FEAT, HID, BLK = 1024, 1792, 128
 SUB = 16
 TILE = 256
-
-DIRECT = (4, 0)
+WIDE = 896
+
+DIRECT = (0, 1)
 
 ORDER = [
-    "I", "L", "A0", "B0", "Z2", "Z1", "C0", "D0", "A6", "Y3", "Y2", "A2", "Y1", "A1", "E0", "B6", "B2", "P6",
-    "Z3", "P2", "B1", "F0", "A4", "M0", "C2", "C6", "B4", "P4", "C1", "D2", "D6", "C4", "A3", "Y5", "A7",
-    "D1", "E2", "B3", "P3", "Y4", "P7", "B7", "E6", "D4", "E1", "F2", "C3", "A5", "P5", "M2", "C7", "J0",
-    "B5", "F6", "E4", "M6", "F1", "D3", "D7", "M1", "C5", "F4", "M4", "E3", "E7", "D5", "G1", "G2", "G6",
-    "F3", "F7", "M3", "M7", "N0", "E5", "H1", "H2", "H6", "G3", "F5", "J1", "G7", "M5", "U6", "V0", "H3",
-    "U4", "U5", "U3", "H7", "J2", "U1", "J3", "U0", "N1", "J4", "J6", "V2", "J7", "V1", "G5", "V3", "v3",
-    "u5", "u6", "Q1", "H5", "u1", "u0", "v0", "v1", "J5", "u4", "v2", "u3", "U2", "u2", "X", "Q0",
+    "I", "L", "A0", "B0", "C0", "Z2", "Z1", "D0", "A2", "P6", "A6", "B2", "Y1", "B6", "A1", "E0", "Z3", "Y3",
+    "C6", "B1", "C2", "F0", "Y2", "C1", "P2", "D6", "D2", "P3", "Y4", "Y5", "D1", "A7", "A3", "B7", "A4",
+    "E6", "E2", "E1", "C7", "B3", "A5", "F6", "F2", "F1", "B5", "B4", "M0", "C3", "M1", "C5", "C4", "M6",
+    "D7", "M2", "D5", "D3", "E5", "P7", "D4", "E7", "E3", "F5", "E4", "P4", "P5", "G6", "F7", "M5", "G2",
+    "F3", "M7", "G3", "F4", "M3", "G7", "U3", "H6", "U2", "V2", "U1", "J0", "N1", "H2", "H3", "V3", "U5",
+    "H7", "G4", "U0", "G5", "V0", "J2", "U6", "J1", "J3", "J6", "M4", "J7", "U4", "V1", "Q1", "H4", "u4",
+    "u6", "H5", "u1", "u0", "v3", "v2", "N0", "J5", "J4", "v0", "u2", "u3", "u5", "v1", "X", "Q0",
 ]
 
 
@@ -186,13 +187,13 @@
         yy, hh = at(u)
 
         def tile(n, carry):
-            cols = pl.ds(pl.multiple_of(n * TILE, TILE), TILE)
-            shape = (2, 4, SUB, TILE)
+            cols = pl.ds(pl.multiple_of(n * WIDE, WIDE), WIDE)
+            shape = (2, 4, SUB, WIDE)
             PP[u, 0, :, :, :, cols] = nn(TC[d, 0, yy, hh], win[:, cols]).astype(BF).reshape(shape)
             PP[u, 1, :, :, :, cols] = nt(TC[d, 1, yy, hh], wout[cols, :]).astype(BF).reshape(shape)
             return carry
 
-        lax.fori_loop(0, HID // TILE, tile, 0)
+        lax.fori_loop(0, HID // WIDE, tile, 0)
         send(f"r1{u}", PP.at[u, :, sib], RB.at[u], to_sib)
 
     def pair(u, kind, q):
@@ -225,7 +226,7 @@
             pair(u, kind, x) + X1[u, 0, kind].astype(F32) + X1[u, 1, kind].astype(F32)
             for kind in range(2)
         ]
-        g = gain[...]
+        g = gain[...].reshape(1, HID)
         scaled = sums[0] * g
         total = jnp.zeros_like(scaled)
         slope = jnp.zeros_like(scaled)
@@ -276,15 +277,10 @@
         k, r = u // 2, u % 2
         yy, hh = at(u)
 
-        def tile(n, carry):
-            cols = pl.ds(pl.multiple_of(n * TILE, TILE), TILE)
-            a = SG[d, 0, yy, hh].reshape(BLK, HID)
-            OP[k, r, 0, :, cols] = nn(a, wout[:, cols]).astype(BF)
-            b = SG[d, 1, yy, hh].reshape(BLK, HID)
-            OP[k, r, 1, :, cols] = nt(b, win[cols, :]).astype(BF)
-            return carry
-
-        lax.fori_loop(0, FEAT // TILE, tile, 0)
+        a = SG[d, 0, yy, hh].reshape(BLK, HID)
+        OP[k, r, 0] = nn(a, wout[...]).astype(BF)
+        b = SG[d, 1, yy, hh].reshape(BLK, HID)
+        OP[k, r, 1] = nt(b, win[...]).astype(BF)
         if k == 2:
             send(f"d2p{r}", OP.at[2, r, 0], YB2.at[r, 0], to_yp)
             send(f"d2m{r}", OP.at[2, r, 1], YB2.at[r, 1], to_ym)
@@ -409,11 +405,49 @@
         sent[name].wait_send()
 
 
+PARTS = ((1, 128), (1, 128), (8, 128), (8, 224))
+
+
+def hand_over_kernel(*refs):
+    ins, outs, bufs, sems = refs[:4], refs[4:8], refs[8:12], refs[12]
+    copies = []
+    i = 0
+    for a, b, o, (n, rows) in zip(ins, bufs, outs, PARTS):
+        for j in range(n):
+            part = pl.ds(j * rows, rows)
+            copies.append((
+                pltpu.make_async_copy(a.at[part], b.at[part], sems.at[i]),
+                pltpu.make_async_copy(b.at[part], o.at[part], sems.at[i + 1]),
+            ))
+            i += 2
+    for load, _ in copies:
+        load.start()
+    for load, keep in copies:
+        load.wait()
+        keep.start()
+    for _, keep in copies:
+        keep.wait()
+
+
+def hand_over(results):
+    anywhere = pl.BlockSpec(memory_space=pl.ANY)
+    return pl.pallas_call(
+        hand_over_kernel,
+        out_shape=tuple(jax.ShapeDtypeStruct(r.shape, r.dtype) for r in results),
+        in_specs=[anywhere] * 4,
+        out_specs=[anywhere] * 4,
+        scratch_shapes=[pltpu.VMEM(r.shape, r.dtype) for r in results]
+        + [pltpu.SemaphoreType.DMA((2 * sum(n for n, _ in PARTS),))],
+        compiler_params=pltpu.CompilerParams(vmem_limit_bytes=63 << 20),
+        name="hand_over",
+    )(*results)
+
+
 def shards(tokens, w_in, w_out, spike_gain, cotangent):
     anywhere = pl.BlockSpec(memory_space=pl.ANY)
     vmem = pltpu.VMEM
     n = len(NAMES)
-    return pl.pallas_call(
+    results = pl.pallas_call(
         kernel,
         out_shape=(
             jax.ShapeDtypeStruct((BLK, FEAT), BF),
@@ -426,7 +460,7 @@
         scratch_shapes=[
             vmem((FEAT, HID), BF),
             vmem((HID, FEAT), BF),
-            vmem((1, HID), F32),
+            vmem((HID,), F32),
             vmem((2, 2, 4, 2, BLK, FEAT), BF),
             vmem((8, 2, 2, 4, SUB, HID), BF),
             vmem((8, 2, 4, SUB, HID), BF),
@@ -449,7 +483,8 @@
             collective_id=0, has_side_effects=True, vmem_limit_bytes=64 << 20
         ),
         name="spiking_block",
-    )(tokens, w_in, w_out, spike_gain.reshape(1, HID), cotangent)
+    )(tokens, w_in, w_out, spike_gain, cotangent)
+    return hand_over(results)
 
 
 def solution(mesh):

time: 142 us -> 123 us (0.87)
  local copies, waits for them, and re-layouts: 10.7 us -> 0 us
  Pallas kernels: 130 us -> 122 us
    pallas_call x1, Pallas kernels: 130 us -> 116 us  [shards(): pl.pallas_call(kernel, out_shape=(jax.ShapeDtypeStruct((BLK, FEAT), BF),...]
    unnamed x6 -> x0, local copies, waits for them, and re-layouts: 9.44 us -> none
    pallas_call x0 -> x1, Pallas kernels: none -> 6.26 us  [hand_over(): pl.pallas_call(hand_over_kernel, out_shape=tuple((jax.ShapeDtypeStruct(r....]
where the time goes in v3:
time: 123 us
  Pallas kernels  122 us (99%)
    pallas_call x1, Pallas kernels, shards(): pl.pallas_call(kernel, out_shape=(jax.ShapeDtypeStruct((BLK, FEAT), BF),...  116 us
    pallas_call x1, Pallas kernels, hand_over(): pl.pallas_call(hand_over_kernel, out_shape=tuple((jax.ShapeDtypeStruct(r....  6.26 us

profile of v3, /device:TPU:0, one launch (start us, length us, event | category | flops | bytes accessed | tf_op | source)
XLA Modules:
  0.0 122.7 jit_solution(4042529650787107399)
XLA Ops:
  0.6 115.6 %spiking_block.1 = (bf16[128,1024]{1,0:T(8,128)(2,1)}, bf16[128,1024]{1,0:T(8,128)(2,1)}, bf16[1024,1792]{1,0:T(8,128)(2,1)}, bf16[1792,1024]{1,0:T(8,128)(2,1)}) custom-call(bf16[128,1024]{1,0:T(8,128)(2,1)} %tok_h.1, bf16[1024,1792]{1,0:T(8,128)(2,1)} %win_h.1, bf16[1792,1024]{1,0:T(8,128)(2,1)} %wout_h.1, f32[1792]{0:T(1024)} %gain_h.1, ...), custom_call_target="tpu_custom_call" | custom-call | tf_op jit(solution)/shard_map/spiking_block/pallas_call | solution.py:450
  116.2 6.3 %hand_over.1 = (bf16[128,1024]{1,0:T(8,128)(2,1)}, bf16[128,1024]{1,0:T(8,128)(2,1)}, bf16[1024,1792]{1,0:T(8,128)(2,1)}, bf16[1792,1024]{1,0:T(8,128)(2,1)}) custom-call(bf16[128,1024]{1,0:T(8,128)(2,1)} %get-tuple-element.8.refs_0_, bf16[128,1024]{1,0:T(8,128)(2,1)} %get-tuple-element.9.refs_1_, bf16[1024,1792]{1,0:T(8,128)(2,1)} %get-tuple-element.10.refs_2_, ...), custom_call_target="tpu_custom_call" | custom-call | tf_op jit(solution)/shard_map/hand_over/pallas_call | solution.py:434
